TPU v7x, 256 devices: a whole 4x4x8 slice. The times are simulated.
256 devices in a mesh: occ: 8 (over z_hi, core), aux: 32 (over x, z_lo, y).
Axes of the slice: x: 4, y: 4, z: 8 (z_hi: 4, z_lo: 2; z = z_hi * 2 + z_lo), core: 2. Of those that a mesh axis runs over, the one named last changes fastest.
Arguments:
- coeffs: bfloat16 [8, 256, 131072], P('occ', None, 'aux'), may hold values from -0.31445312 to 0.31445312
- occ_energy: bfloat16 [8], P('occ'), may hold values from -1.5 to -0.29882812
- virt_energy: bfloat16 [256], replicated, may hold values from 0.19921875 to 3
- screen: int32 [8, 1024], P('occ', 'aux'), may hold values 0 or 1
- owner: int32 [1024], P('aux'), may hold values from 0 to 127
- positions: float32 [3, 128], replicated, may hold values from -1 to 1
Outputs:
- gamma: bfloat16 [8, 256, 131072], P('occ', None, 'aux')
- virial: float32 [9, 131072], P(None, 'aux')
All inputs are finite; a program needn't handle non-finite values. No bound on the sum of `screen` on one device may be relied on, other than what follows from the above.
Results may differ from a plain program's by a relative error of at most 0.0049.
Values may be sent and summed in bfloat16 or wider, within the bound.
A program may use at most 64 MiB of HBM per device.

v0:
```python
import jax
import jax.numpy as jnp
from jax import lax
from jax.sharding import PartitionSpec as P

ABLK = 128


def body(coeffs, occ_energy, virt_energy, screen, owner, positions):
    occ_dev, virt, aux_dev = coeffs.shape
    column_mask = jnp.repeat(screen[0], ABLK).astype(jnp.bfloat16)
    masked = coeffs * column_mask[None, None, :]
    whole, energies = (
        lax.all_gather(masked, "occ", axis=0, tiled=True),
        lax.all_gather(occ_energy, "occ", axis=0, tiled=True),
    )
    all_rows = whole.reshape(-1, aux_dev)
    local = masked.reshape(-1, aux_dev)
    virt_f = virt_energy.astype(jnp.float32)
    spread_local = (virt_f[None, :] - occ_energy.astype(jnp.float32)[:, None]).reshape(-1)
    spread_all = (virt_f[None, :] - energies.astype(jnp.float32)[:, None]).reshape(-1)
    contract_last = (((1,), (1,)), ((), ()))
    contract_first = (((0,), (0,)), ((), ()))
    summed = lax.psum(
        lax.dot_general(all_rows, local, contract_last, preferred_element_type=jnp.float32), "aux"
    )
    amps = (summed / (spread_all[:, None] + spread_local[None, :])).astype(jnp.bfloat16)
    gamma = lax.dot_general(amps, all_rows, contract_first, preferred_element_type=jnp.float32)
    gamma_out = gamma.astype(jnp.bfloat16)
    partial_weight = jnp.sum(gamma_out.astype(jnp.float32) * local.astype(jnp.float32), axis=0)
    weight = lax.psum(partial_weight, "occ")
    atom_ids = jnp.arange(positions.shape[1], dtype=jnp.int32)
    onehot = (owner[:, None] == atom_ids[None, :]).astype(jnp.float32)
    block_where = jnp.dot(onehot, positions.T, precision=lax.Precision.HIGHEST)
    where = jnp.repeat(block_where.T, ABLK, axis=1)
    virial = (where[:, None, :] * where[None, :, :]).reshape(9, aux_dev) * weight[None, :]
    return (gamma_out.reshape(occ_dev, virt, aux_dev), virial)


def solution(mesh):
    placed = (P("occ", None, "aux"), P("occ"), P(), P("occ", "aux"), P("aux"), P())
    return jax.shard_map(
        body,
        mesh=mesh,
        in_specs=placed,
        out_specs=(P("occ", None, "aux"), P(None, "aux")),
        check_vma=False,
    )
```

profile of v0, /device:TPU:1, one launch (start us, length us, event | category | flops | bytes accessed | tf_op | source)
XLA Modules:
  0.0 543.2 jit_solution(9232543608155774374)
XLA Ops:
  7.2 0.0 copy-start
  7.2 0.0 all-gather.2.cloned.1.call-start
  7.2 0.7 convert_bitcast_fusion
  7.9 0.1 broadcast_bitcast_fusion.1
  8.0 3.1 broadcast_multiply_fusion
  11.0 0.0 copy-start.1
  11.0 0.0 all-gather.2.cloned.1.call-update
  11.0 0.0 all-reduce.3.cloned.1.call-start
  11.1 161.0 %all-gather.2.cloned.1.call-done = bf16[8,256,4096]{2,1,0:T(8,128)(2,1)} async-done(((bf16[1,256,4096]{2,1,0:T(8,128)(2,1)}), bf16[8,256,4096]{2,1,0:T(8,128)(2,1)}) %all-gather.2.cloned.1.call-update) | async-done | bytes 16777232 | tf_op jit(solution)/shard_map/all_gather | solution.py:14
  172.1 0.0 copy-done.1
  172.1 9.6 %fusion = f32[2048,256]{1,0:T(8,128)} fusion(bf16[2048,4096]{1,0:T(8,128)(2,1)} %bitcast.29, bf16[1,256,4096]{2,1,0:T(8,128)(2,1)S(1)} %copy-done.1), kind=kOutput, calls=%fused_computation.2 | convolution fusion | flops 4294967296 | bytes 20971520 | tf_op jit(solution)/shard_map/dot_general | solution.py:25
  181.7 0.0 copy-start.4
  181.7 0.0 copy-start.2
  181.7 0.0 copy-start.3
  181.7 0.0 all-reduce.3.cloned.1.call-update
  182.4 0.0 copy-done.4
  182.4 0.6 dynamic-slice
  183.0 0.7 dynamic-update-slice
  183.7 13.8 %all-reduce = bf16[8]{0:T(256)(128)(2,1)S(1)} all-reduce(bf16[8]{0:T(256)(128)(2,1)S(1)} %dynamic-update-slice), channel_id=1, replica_groups=mesh['occ'=8,'aux'=32] {'occ'}, use_global_device_ids=true, to_apply=%add | all-reduce | flops 8 | bytes 32
  197.6 0.0 copy-done.2
  197.6 0.1 subtract_bitcast_fusion
  197.7 0.0 copy-done
  197.7 0.0 copy-done.3
  197.7 0.2 convolution_bitcast_fusion
  197.9 0.1 broadcast_bitcast_fusion
  197.9 0.1 copy.11
  198.1 0.1 mul.44
  198.1 278.2 %all-reduce.3.cloned.1.call-done = f32[2048,256]{1,0:T(8,128)} async-done(((f32[2048,256]{1,0:T(8,128)}), f32[2048,256]{1,0:T(8,128)}) %all-reduce.3.cloned.1.call-update) | async-done | bytes 2097168 | tf_op jit(solution)/shard_map/psum | solution.py:24
  476.3 12.8 %multiply_reduce_fusion = (f32[4096]{0:T(1024)S(1)}, bf16[256,4096]{1,0:T(8,128)(2,1)}) fusion(bf16[1,256,4096]{2,1,0:T(8,128)(2,1)S(1)} %copy-done.1, bf16[2048,4096]{1,0:T(8,128)(2,1)} %bitcast.30, f32[2048,256]{1,0:T(8,128)} %all-reduce.3.cloned.1.call-done, f32[256]{0:T(256)S(1)} %broadcast_subtract_fusion, f32[2048]{0:T(1024)S(1)} %bitcast.28), kind=kOutput, calls=%fused_computation.1 | convolution fusion | flops 4301778944 | bytes 23094272 | tf_op jit(solution)/shard_map/dot_general | solution.py:28
  489.1 46.5 %psum.15 = f32[4096]{0:T(1024)S(1)} all-reduce(f32[4096]{0:T(1024)S(1)} %get-tuple-element.2), channel_id=1, replica_groups=mesh['occ'=8,'aux'=32] {'occ'}, use_global_device_ids=true, to_apply=%region_2.0 | all-reduce | flops 4096 | bytes 32768 | tf_op jit(solution)/shard_map/psum | solution.py:31
  535.7 0.7 broadcast_multiply_fusion.1
  (6 shorter events, 0.1 us)
Async XLA Ops:
  7.2 190.5 %copy-start = (f32[3,128]{1,0:T(4,128)S(1)}, f32[3,128]{1,0:T(4,128)}, u32[]{:S(2)}) copy-start(f32[3,128]{1,0:T(4,128)} %param.11) | copy-start | bytes 4612
  7.2 164.9 %all-gather.2.cloned.1.call-start = ((), (), s32[]{:S(2)}) async-start(), calls=%async_computation | async-start | bytes 18874368 | tf_op jit(solution)/shard_map/all_gather | solution.py:14
  11.0 161.1 %copy-start.1 = (bf16[1,256,4096]{2,1,0:T(8,128)(2,1)S(1)}, bf16[1,256,4096]{2,1,0:T(8,128)(2,1)}, u32[]{:S(2)}) copy-start(bf16[1,256,4096]{2,1,0:T(8,128)(2,1)} %broadcast_multiply_fusion) | copy-start | bytes 6291460
  11.0 465.3 %all-reduce.3.cloned.1.call-start = ((), (), s32[]{:S(2)}) async-start(), calls=%async_computation.1 | async-start | bytes 4194304 | tf_op jit(solution)/shard_map/psum | solution.py:24
  181.7 0.7 copy-start.4
  181.7 15.9 %copy-start.2 = (bf16[256]{0:T(256)(128)(2,1)S(1)}, bf16[256]{0:T(256)(128)(2,1)}, u32[]{:S(2)}) copy-start(bf16[256]{0:T(256)(128)(2,1)} %param.8) | copy-start | bytes 1540
  181.7 15.9 %copy-start.3 = (s32[32]{0:T(128)S(1)}, s32[32]{0:T(128)}, u32[]{:S(2)}) copy-start(s32[32]{0:T(128)} %param.10) | copy-start | bytes 388
Sparse Core Ops, SparseCore 0:
  11.2 160.8 all-gather.1
  181.9 294.4 all-reduce.2
where the time goes:
time: 545 us; the launch traced here: 543 us
  waiting for transfers between devices  439 us (81%)
  blocking collectives  60.4 us (11%)
  matrix products  22.6 us (4%)
  between operations  14.8 us (3%)
    psum x1, waiting for transfers between devices, body(): lax.psum(lax.dot_general(all_rows, local, contract_last, preferred_elemen...  278 us
    all_gather x1, waiting for transfers between devices, body(): lax.all_gather(masked, 'occ', axis=0, tiled=True)  161 us
    psum x1, blocking collectives, body(): weight = lax.psum(partial_weight, 'occ')  46.5 us
    unnamed x1, blocking collectives  13.8 us
    dot_general x1, matrix products, body(): lax.dot_general(amps, all_rows, contract_first, preferred_element_type=jn...  12.8 us
  transfers between devices with their start and end apart: 2, of which 2 were waited for; matrix products, arithmetic and copies ran while one was open for 0% of the time, Pallas kernels for 0%

commit v1 on v0

v1 whole, which is shorter than its diff:
```python
import functools

import jax
import jax.numpy as jnp
from jax import lax
from jax.experimental import pallas as pl
from jax.experimental.pallas import tpu as pltpu
from jax.sharding import PartitionSpec as P

MESH = pl.DeviceIdType.MESH
F32, BF16 = jnp.float32, jnp.bfloat16

ABLK = 128
VIRT = 256
COLS = 512
TAIL = 16
CHUNK = 16
NBLK = 10
EARLY = 6

SLOTS = ((0, 0), (1, 1), (3, 3), (0, 1), (3, 0), (1, 3), (2, 2), (1, 2), (2, 3), (0, 2))
GROUPS = ((0, EARLY), (EARLY, NBLK))


def dot_nt(a, b):
    return lax.dot_general(a, b, (((1,), (1,)), ((), ())), preferred_element_type=F32)


def dot_nn(a, b):
    return lax.dot_general(a, b, (((1,), (0,)), ((), ())), preferred_element_type=F32)


def dot_tn(a, b):
    return lax.dot_general(a, b, (((0,), (0,)), ((), ())), preferred_element_type=F32)


def kernel(
    coeffs, mask, energy, vrow, vcol, owner, atoms,
    gamma, virial,
    slabs, rows, part, plane_in, plane_sum, z_in, z_amps, amps, turned, gout, wmine, wall, where,
    sa, ra, sf, rf, sp, rp, sz, rz, sy, ry, sg, rg, sh, rh, sb, rb, sw, rw,
):
    o = lax.axis_index("occ")
    a = lax.axis_index("aux")
    c, h = o // 2, o % 2
    y, zl, x = a % 4, (a // 4) % 2, a // 8
    z = c * 2 + zl
    q = x * 4 + y
    other = 1 - h

    def at(x_, y_, z_, h_):
        return {"occ": (z_ // 2) * 2 + h_, "aux": (x_ * 2 + z_ % 2) * 4 + y_}

    partner = at(x, y, z, other)
    occ_peers = {}
    for dc in (1, 3, 2):
        for dh in (0, 1):
            occ_peers[dc, dh] = at(x, y, (z + 2 * dc) % 8, (h + dh) % 2)
    plane_peers = {}
    for dx in range(4):
        for dy in range(4):
            if (dx, dy) != (0, 0):
                plane_peers[dx * 4 + dy] = (
                    at((x + dx) % 4, (y + dy) % 4, z, h),
                    ((x + dx) % 4) * 4 + (y + dy) % 4,
                )
    z_peers = {dz: (at(x, y, (z + dz) % 8, h), (z + dz) % 8) for dz in range(1, 8)}

    barrier = pltpu.get_barrier_semaphore()
    greet = [partner, *occ_peers.values()]
    greet += [d for d, _ in plane_peers.values()]
    greet += [d for dz, (d, _) in z_peers.items() if dz % 2]
    for d in greet:
        pl.semaphore_signal(barrier, inc=1, device_id=d, device_id_type=MESH)

    sent = []

    def send(src, dst, ss, rs, d):
        cp = pltpu.make_async_remote_copy(
            src_ref=src, dst_ref=dst, send_sem=ss, recv_sem=rs, device_id=d, device_id_type=MESH
        )
        cp.start()
        sent.append(cp)
        return cp

    def mask_slab(k, _):
        cols = pl.ds(pl.multiple_of(k * COLS, COLS), COLS)
        slabs[k, 0:VIRT, :] = coeffs[:, cols] * mask[:, cols]
        slabs[k, VIRT:, :] = energy[...]
        return 0

    lax.fori_loop(0, 8, mask_slab, 0)

    def keep_slab(half, _):
        rows[o, half] = slabs[c * 2 + half]
        return 0

    lax.fori_loop(0, 2, keep_slab, 0)

    pl.semaphore_wait(barrier, len(greet))

    to_partner = send(rows.at[o], rows.at[o], sa.at[6], ra.at[6], partner)
    slab_in = {}
    for n, (key, d) in enumerate(occ_peers.items()):
        dc, dh = key
        dst_o = ((c + dc) % 4) * 2 + (h + dh) % 2
        slab_in[key] = send(slabs.at[dst_o], rows.at[o, (h + dh) % 2], sa.at[n], ra.at[n], d)

    def place(k, _):
        cols = pl.ds(pl.multiple_of(k * COLS, COLS), COLS)
        ids = lax.broadcasted_iota(jnp.int32, (128, COLS), 0)
        onehot = (ids == owner[:, cols]).astype(F32)
        where[:, cols] = lax.dot_general(
            atoms[...], onehot, (((1,), (0,)), ((), ())),
            precision=lax.Precision.HIGHEST, preferred_element_type=F32,
        )
        return 0

    lax.fori_loop(0, 8, place, 0)

    def product(slot):
        r0, r1 = SLOTS[slot]
        first, second = (c + r0) % 4, (c + r1) % 4
        if slot in (5, 9):
            first, second = jnp.minimum(first, second), jnp.maximum(first, second)
        lead = first * 2 + h

        def column(hc, _):
            co = second * 2 + hc
            s = dot_nt(rows[lead, 0, 0:VIRT], rows[co, 0, 0:VIRT])
            s += dot_nt(rows[lead, 1, 0:VIRT], rows[co, 1, 0:VIRT])
            part[slot, :, pl.ds(pl.multiple_of(hc * VIRT, VIRT), VIRT)] = s.astype(BF16)
            return 0

        lax.fori_loop(0, 2, column, 0)

    def pass_on(keys):
        out = []
        for key in keys:
            dc, dh = key
            n = list(occ_peers).index(key)
            slab_in[key].wait_recv()
            src_o = ((c + 4 - dc) % 4) * 2 + (h + dh) % 2
            out.append(send(rows.at[src_o, h], rows.at[src_o, h], sf.at[n], rf.at[n], partner))
        for cp in out:
            cp.wait_recv()

    plane_wait = {}

    def share_products(g):
        lo, hi = GROUPS[g]
        for j, (d, qd) in plane_peers.items():
            there = pl.ds(pl.multiple_of(qd * CHUNK, CHUNK), CHUNK)
            plane_wait[g, j] = send(
                part.at[lo:hi, there, :], plane_in.at[j, lo:hi], sp.at[g, j], rp.at[g, j], d
            )

    mine = pl.ds(pl.multiple_of(q * CHUNK, CHUNK), CHUNK)

    def block_id(slot):
        r0, r1 = SLOTS[slot]
        if r0 == r1:
            return (c + r0) % 4
        if slot in (5, 9):
            return 8 + (c + r0) % 2
        return 4 + (c + r0) % 4

    def sum_plane(g):
        lo, hi = GROUPS[g]
        for j in plane_peers:
            plane_wait[g, j].wait_recv()
        for slot in range(lo, hi):
            s = part[slot, mine, :].astype(F32)
            for j in plane_peers:
                s += plane_in[j, slot].astype(F32)
            plane_sum[block_id(slot)] = s

    to_partner.wait_recv()
    product(0)
    pass_on([(1, 0), (1, 1), (3, 0), (3, 1)])
    for slot in range(1, EARLY):
        product(slot)
    share_products(0)
    pass_on([(2, 0), (2, 1)])
    for slot in range(EARLY, NBLK):
        product(slot)
    share_products(1)
    sum_plane(0)
    sum_plane(1)

    def share_of(k):
        return (
            pl.ds((k // 4) * 5, 5),
            slice(None),
            pl.ds(pl.multiple_of((k % 4) * 128, 128), 128),
        )

    z_wait = {}
    for dz, (d, zd) in z_peers.items():
        z_wait[dz] = send(plane_sum.at[share_of(zd)], z_in.at[dz], sz.at[dz], rz.at[dz], d)
    for dz in z_peers:
        z_wait[dz].wait_recv()

    hc = (z % 4) // 2
    va = vrow[mine, :]
    vb = vcol[:, pl.ds(pl.multiple_of((z % 2) * 128, 128), 128)]
    lanes = pl.ds(pl.multiple_of((z % 4) * 128, 128), 128)
    for t in range(5):
        b = (z // 4) * 5 + t
        s = plane_sum[b, :, lanes]
        for dz in z_peers:
            s += z_in[dz, t]
        near = b % 4
        lead = near * 2 + h
        far = jnp.where(b < 4, near, jnp.where(b < 8, (near + 1) % 4, near + 2))
        ea = rows[lead, h, VIRT:, 0:128].astype(F32)
        eb = rows[far * 2 + hc, h, VIRT:, 0:128].astype(F32)
        z_amps[b, :, lanes] = (s / ((va - ea) + (vb - eb))).astype(BF16)
    y_wait = {}
    for dz, (d, _) in z_peers.items():
        y_wait[dz] = send(
            z_amps.at[share_of(z)], z_amps.at[share_of(z)], sy.at[dz], ry.at[dz], d
        )
    for dz in z_peers:
        y_wait[dz].wait_recv()

    here = pl.ds(pl.multiple_of(h * VIRT + q * CHUNK, CHUNK), CHUNK)
    for slot in range(NBLK):
        amps[slot, here, :] = z_amps[block_id(slot)]
    g_wait = {}
    for g in (1, 0):
        lo, hi = GROUPS[g]
        piece = amps.at[lo:hi, here, :]
        g_wait[g, 0] = send(piece, piece, sh.at[g, 0], rh.at[g, 0], partner)
        for j, (d, _) in plane_peers.items():
            g_wait[g, j] = send(piece, piece, sg.at[g, j], rg.at[g, j], d)

    def collect(g):
        lo, hi = GROUPS[g]
        out = [g_wait[g, 0]]
        for j in plane_peers:
            dx, dy = j // 4, j % 4
            src_q = ((x + 4 - dx) % 4) * 4 + (y + 4 - dy) % 4
            g_wait[g, j].wait_recv()
            piece = amps.at[lo:hi, pl.ds(pl.multiple_of(h * VIRT + src_q * CHUNK, CHUNK), CHUNK), :]
            out.append(send(piece, piece, sh.at[g, j], rh.at[g, j], partner))
        for cp in out:
            cp.wait_recv()
        n = 1 - g
        slot, low = ((9, c < 2), (5, (c + 1) % 4 < 2))[n]

        @pl.when(low)
        def _():
            turned[n] = amps[slot]

        @pl.when(jnp.logical_not(low))
        def _():
            turned[n] = amps[slot].T

    def factor(r, rc, hr):
        span = pl.ds(pl.multiple_of(hr * VIRT, VIRT), VIRT)
        for slot, pair in enumerate(SLOTS):
            ref = turned.at[0] if slot == 9 else turned.at[1] if slot == 5 else amps.at[slot]
            if pair == (r, rc):
                return dot_nn, ref, (span, None)
            if pair == (rc, r):
                return dot_tn, ref, (None, span)
        raise AssertionError

    weight = jnp.zeros((1, COLS), F32)
    b_wait = {}

    def gamma_rows(r, dh, weight):
        hr = (h + dh) % 2
        ro = ((c + r) % 4) * 2 + hr
        acc = None
        for rc in range(4):
            dot, ref, (rs, cs) = factor(r, rc, hr)
            for hcol in range(2):
                half = slice(hcol * VIRT, (hcol + 1) * VIRT)
                block = ref[rs, half] if cs is None else ref[half, cs]
                term = dot(block, rows[((c + rc) % 4) * 2 + hcol, h, 0:VIRT])
                acc = term if acc is None else acc + term
        out = acc.astype(BF16)
        weight += jnp.sum(out.astype(F32) * rows[ro, h, 0:VIRT].astype(F32), axis=0, keepdims=True)
        cols = pl.ds(pl.multiple_of(o * COLS, COLS), COLS)
        if (r, dh) == (0, 0):
            gamma[:, cols] = out
        else:
            gout[ro] = out
            d = partner if r == 0 else occ_peers[r, dh]
            n = r * 2 + dh
            b_wait[n] = send(gout.at[ro], gamma.at[:, cols], sb.at[n], rb.at[n], d)
        return weight

    collect(1)
    for dh in (0, 1):
        weight = gamma_rows(2, dh, weight)
    collect(0)
    for r in (1, 3, 0):
        for dh in (1, 0):
            weight = gamma_rows(r, dh, weight)

    wmine[...] = jnp.broadcast_to(weight, (8, COLS))
    wall[o] = jnp.broadcast_to(weight, (8, COLS))
    w_wait = [send(wmine, wall.at[o], sw.at[6], rw.at[6], partner)]
    for n, d in enumerate(occ_peers.values()):
        w_wait.append(send(wmine, wall.at[o], sw.at[n], rw.at[n], d))
    for cp in w_wait:
        cp.wait_recv()

    def terms(k, _):
        cols = pl.ds(pl.multiple_of(k * COLS, COLS), COLS)
        w = wall[k, 0:1, :]
        for i in range(3):
            for j in range(3):
                virial[3 * i + j : 3 * i + j + 1, cols] = where[i : i + 1, cols] * where[j : j + 1, cols] * w
        return 0

    lax.fori_loop(0, 8, terms, 0)
    for cp in b_wait.values():
        cp.wait_recv()
    for cp in sent:
        cp.wait_send()


def body(coeffs, occ_energy, virt_energy, screen, owner, positions):
    occ_dev, virt, aux_dev = coeffs.shape
    mask = jnp.repeat(screen, ABLK, axis=1).astype(BF16)
    owners = jnp.repeat(owner[None, :], ABLK, axis=1)
    energy = jnp.broadcast_to(occ_energy[:, None], (TAIL, COLS))
    virt_f = virt_energy.astype(F32)
    vrow = jnp.broadcast_to(virt_f[:, None], (VIRT, 128))
    vcol = jnp.broadcast_to(virt_f[None, :], (CHUNK, VIRT))
    atoms = jnp.pad(positions, ((0, 5), (0, 0)))
    vmem = pl.BlockSpec(memory_space=pltpu.VMEM)
    dma = pltpu.SemaphoreType.DMA
    gamma, virial = pl.pallas_call(
        kernel,
        out_shape=(
            jax.ShapeDtypeStruct((VIRT, aux_dev), BF16),
            jax.ShapeDtypeStruct((9, aux_dev), F32),
        ),
        in_specs=[vmem] * 7,
        out_specs=(vmem, vmem),
        scratch_shapes=[
            pltpu.VMEM((8, VIRT + TAIL, COLS), BF16),
            pltpu.VMEM((8, 2, VIRT + TAIL, COLS), BF16),
            pltpu.VMEM((NBLK, VIRT, 2 * VIRT), BF16),
            pltpu.VMEM((16, NBLK, CHUNK, 2 * VIRT), BF16),
            pltpu.VMEM((NBLK, CHUNK, 2 * VIRT), F32),
            pltpu.VMEM((8, 5, CHUNK, 128), F32),
            pltpu.VMEM((NBLK, CHUNK, 2 * VIRT), BF16),
            pltpu.VMEM((NBLK, 2 * VIRT, 2 * VIRT), BF16),
            pltpu.VMEM((2, 2 * VIRT, 2 * VIRT), BF16),
            pltpu.VMEM((8, VIRT, COLS), BF16),
            pltpu.VMEM((8, COLS), F32),
            pltpu.VMEM((8, 8, COLS), F32),
            pltpu.VMEM((8, aux_dev), F32),
            dma((7,)), dma((7,)), dma((6,)), dma((6,)),
            dma((2, 16)), dma((2, 16)), dma((8,)), dma((8,)), dma((8,)), dma((8,)),
            dma((2, 16)), dma((2, 16)), dma((2, 16)), dma((2, 16)),
            dma((8,)), dma((8,)), dma((7,)), dma((7,)),
        ],
        compiler_params=pltpu.CompilerParams(
            collective_id=0, has_side_effects=True, vmem_limit_bytes=60 * 1024 * 1024
        ),
    )(coeffs.reshape(VIRT, aux_dev), mask, energy, vrow, vcol, owners, atoms)
    return gamma.reshape(occ_dev, virt, aux_dev), virial


def solution(mesh):
    placed = (P("occ", None, "aux"), P("occ"), P(), P("occ", "aux"), P("aux"), P())
    return jax.shard_map(
        body,
        mesh=mesh,
        in_specs=placed,
        out_specs=(P("occ", None, "aux"), P(None, "aux")),
        check_vma=False,
    )
```

time: 545 us -> 195 us (0.36)
  waiting for transfers between devices: 439 us -> 0 us
  Pallas kernels: 0 us -> 183 us
  blocking collectives: 60.4 us -> 0 us
  matrix products: 22.6 us -> 0 us
  between operations: 14.8 us -> 1.31 us
  local copies, waits for them, and re-layouts: 1.64 us -> 10.4 us
    psum x1 -> x0, waiting for transfers between devices: 278 us -> none  [body(): lax.psum(lax.dot_general(all_rows, local, contract_last, preferred_elemen...]
    pallas_call x0 -> x1, Pallas kernels: none -> 183 us  [body(): pl.pallas_call(kernel, out_shape=(jax.ShapeDtypeStruct((VIRT, aux_dev), B...]
    all_gather x1 -> x0, waiting for transfers between devices: 161 us -> none  [body(): lax.all_gather(masked, 'occ', axis=0, tiled=True)]
    psum x1 -> x0, blocking collectives: 46.5 us -> none  [body(): weight = lax.psum(partial_weight, 'occ')]
    dot_general x3 -> x0, matrix products: 22.6 us -> none  [the longest x1 12.8 us: body(): lax.dot_general(amps, all_rows, contract_first, preferred_element_type=jn...]
    unnamed x1 -> x0, blocking collectives: 13.8 us -> none
  transfers between devices with their start and end apart: 2 -> 0, of which waited for: 2 -> 0; matrix products, arithmetic and copies ran while one was open for 0% -> 0% of each run, Pallas kernels for 0% -> 0%
where the time goes in v1:
time: 195 us
  Pallas kernels  183 us (94%)
  local copies, waits for them, and re-layouts  10.4 us (5%)
    pallas_call x1, Pallas kernels, body(): pl.pallas_call(kernel, out_shape=(jax.ShapeDtypeStruct((VIRT, aux_dev), B...  183 us
    unnamed x6, local copies, waits for them, and re-layouts  4.57 us

profile of v1, /device:TPU:1, one launch (start us, length us, event | category | flops | bytes accessed | tf_op | source)
XLA Modules:
  0.0 195.1 jit_solution(7872202667242436177)
XLA Ops:
  1.3 0.7 convert_bitcast_fusion
  1.9 1.3 pad.4.atoms
  3.2 0.1 broadcast_bitcast_fusion
  3.3 0.6 copy.10
  3.9 0.6 broadcast_in_dim.31.energy
  4.5 1.3 broadcast_in_dim.34
  5.8 1.3 broadcast_in_dim.33.vcol
  7.1 1.4 broadcast_in_dim.32.vrow
  8.5 182.7 %shard_map.77 = (bf16[256,4096]{1,0:T(8,128)(2,1)}, f32[9,4096]{1,0:T(8,128)}) custom-call(bf16[256,4096]{1,0:T(8,128)(2,1)} %bitcast.13, bf16[1,4096]{1,0:T(2,128)(2,1)} %bitcast.15, bf16[16,512]{1,0:T(8,128)(2,1)} %broadcast_in_dim.31.energy, f32[256,128]{1,0:T(8,128)} %broadcast_in_dim.32.vrow, f32[16,256]{1,0:T(8,128)} %broadcast_in_dim.33.vcol, ...), custom_call_target="tpu_custom_call" | custom-call | tf_op jit(solution)/shard_map/pallas_call | solution.py:338
  191.2 0.0 copy-start
  191.2 3.2 %copy.14 = bf16[1,256,4096]{2,1,0:T(8,128)(2,1)} copy(bf16[1,256,4096]{2,1,0:T(8,128)(2,1)} %bitcast.14) | data formatting | bytes 4194304
  194.4 0.0 copy-done
  194.4 0.7 copy.15
Async XLA Ops:
  191.2 3.2 %copy-start = (f32[9,4096]{1,0:T(8,128)S(1)}, f32[9,4096]{1,0:T(8,128)}, u32[]{:S(2)}) copy-start(f32[9,4096]{1,0:T(8,128)} %get-tuple-element.9) | copy-start | bytes 442372

commit v2 on v1

v2 whole, which is shorter than its diff:
```python
import jax
import jax.numpy as jnp
from jax import lax
from jax.experimental import pallas as pl
from jax.experimental.pallas import tpu as pltpu
from jax.sharding import PartitionSpec as P

MESH = pl.DeviceIdType.MESH
F32, BF16 = jnp.float32, jnp.bfloat16

ABLK = 128
VIRT = 256
COLS = 512
TAIL = 16
CHUNK = 16
NBLK = 10
EARLY = 6

SLOTS = ((0, 0), (1, 1), (3, 3), (0, 1), (3, 0), (1, 3), (1, 2), (2, 3), (0, 2), (2, 2))
OPEN = (5, 8)
GROUPS = ((0, EARLY), (EARLY, NBLK))
SPREADS = ((1, 8), (8, 9), (0, 1))


def dot_nt(a, b):
    return lax.dot_general(a, b, (((1,), (1,)), ((), ())), preferred_element_type=F32)


def dot_nn(a, b):
    return lax.dot_general(a, b, (((1,), (0,)), ((), ())), preferred_element_type=F32)


def dot_tn(a, b):
    return lax.dot_general(a, b, (((0,), (0,)), ((), ())), preferred_element_type=F32)


def kernel(
    screen, owner, coeffs, energies, positions,
    gamma, virial,
    raw, slabs, rows, also, vrow, part, plane_in, plane_sum, z_in, z_amps, amps, turned, gout,
    wmine, wall, where,
    sl, sa, ra, sr, rr, st, rt, sf, rf, sm, rm, sp, rp, sz, rz, sy, ry, sg, rg, sh, rh, sb, rb, sw, rw,
):
    o = lax.axis_index("occ")
    a = lax.axis_index("aux")
    c, h = o // 2, o % 2
    y, zl, x = a % 4, (a // 4) % 2, a // 8
    z = c * 2 + zl
    q = x * 4 + y
    other = 1 - h
    side = 1 - 2 * h

    def chip(n):
        return (c + n + 8) % 4

    def at(x_, y_, z_, h_):
        return {"occ": (z_ // 2) * 2 + h_, "aux": (x_ * 2 + z_ % 2) * 4 + y_}

    partner = at(x, y, z, other)
    def on_ring(chip_, h_):
        return at(x, y, chip_ * 2 + zl, h_)

    buddy = on_ring(chip(-side), other)
    buddy_o = chip(-side) * 2 + other
    near = {}
    far = {}
    for flip in (0, 1):
        there = (h + flip) % 2
        for way in (0, 1):
            to = chip(side if way == 0 else -side)
            near[way, flip] = (on_ring(to, there), to * 2 + there)
        far[flip] = (on_ring(chip(2 * there - 1), there), chip(2) * 2 + 1 - there)
    plane_peers = {}
    for dx in range(4):
        for dy in range(4):
            if (dx, dy) != (0, 0):
                plane_peers[dx * 4 + dy] = (
                    at((x + dx) % 4, (y + dy) % 4, z, h),
                    ((x + dx) % 4) * 4 + (y + dy) % 4,
                )
    z_peers = {dz: (at(x, y, (z + dz) % 8, h), (z + dz) % 8) for dz in range(1, 8)}

    barrier = pltpu.get_barrier_semaphore()
    everyone = [partner, *(d for d, _ in near.values()), on_ring(chip(2), h), on_ring(chip(2), other)]
    greet = [*everyone]
    greet += [d for d, _ in plane_peers.values()]
    greet += [d for dz, (d, _) in z_peers.items() if dz % 2]
    for d in greet:
        pl.semaphore_signal(barrier, inc=1, device_id=d, device_id_type=MESH)

    sent = []

    def send(src, dst, ss, rs, d):
        cp = pltpu.make_async_remote_copy(
            src_ref=src, dst_ref=dst, send_sem=ss, recv_sem=rs, device_id=d, device_id_type=MESH
        )
        cp.start()
        sent.append(cp)
        return cp

    order = [t for _, t in near.values()] + [t for _, t in far.values()] + [c * 2 + other, o]
    loads = []
    for n, t in enumerate(order):
        cols = pl.ds(pl.multiple_of(t * COLS, COLS), COLS)
        loads.append(pltpu.make_async_copy(coeffs.at[:, cols], raw.at[n], sl.at[n]))
        loads[n].start()

    energy = jnp.broadcast_to(energies[2:3, :], (TAIL, 128)).astype(BF16)
    near_in, far_in = {}, {}
    for n, t in enumerate(order):
        to = slabs.at[n] if n < 6 else rows.at[o, t % 2]
        loads[n].wait()
        for b in range(COLS // ABLK):
            cols = slice(b * ABLK, (b + 1) * ABLK)
            keep = screen[0, t * (COLS // ABLK) + b].astype(F32)
            kept = raw[n, :, cols] * jnp.full((VIRT, ABLK), keep, F32).astype(BF16)
            to[0:VIRT, cols] = kept
            to[VIRT:, cols] = energy
            if n == 3:
                also[o, 0:VIRT, cols] = kept
        if n == 0:
            pl.semaphore_wait(barrier, len(greet))
        if n < 4:
            key = list(near)[n]
            near_in[key] = send(slabs.at[n], rows.at[o, t % 2], sa.at[n], ra.at[n], near[key][0])
        elif n < 6:
            far_in[n - 4] = send(slabs.at[n], also.at[o], sr.at[n - 4], rr.at[n - 4], far[n - 4][0])
    to_partner = send(rows.at[o], rows.at[o], sa.at[4], ra.at[4], partner)
    also_in = send(slabs.at[0], also.at[o], sa.at[5], ra.at[5], partner)

    for half in (0, 1):
        vrow[half * 128 : (half + 1) * 128, :] = jnp.broadcast_to(
            energies[half : half + 1, :], (128, 128)
        ).T
    atom = lax.broadcasted_iota(jnp.int32, (3, 128), 1)
    for b in range(owner.shape[0]):
        spot = jnp.sum(jnp.where(atom == owner[b], positions[...], 0.0), axis=1, keepdims=True)
        where[0:3, b * ABLK : (b + 1) * ABLK] = jnp.broadcast_to(spot, (3, ABLK))
    pick = (
        lax.broadcasted_iota(jnp.int32, (CHUNK, 16 * CHUNK), 1) % CHUNK
        == lax.broadcasted_iota(jnp.int32, (CHUNK, 16 * CHUNK), 0)
    ).astype(F32).astype(BF16)

    def product(slot):
        r0, r1 = SLOTS[slot]
        first, second = (c + r0) % 4, (c + r1) % 4
        if slot in OPEN:
            first, second = jnp.minimum(first, second), jnp.maximum(first, second)
        lead = first * 2 + h
        for hc in (0, 1):
            s = dot_nt(rows[lead, 0, 0:VIRT], rows[second * 2 + hc, 0, 0:VIRT])
            s += dot_nt(rows[lead, 1, 0:VIRT], rows[second * 2 + hc, 1, 0:VIRT])
            part[slot, :, hc * VIRT : (hc + 1) * VIRT] = s.astype(BF16)

    def pass_on(n, came, src):
        came.wait_recv()
        piece = rows.at[src, h]
        return send(piece, piece, sf.at[n], rf.at[n], partner)

    plane_wait = {}

    def share_products(g):
        lo, hi = GROUPS[g]
        for j, (d, qd) in plane_peers.items():
            there = pl.ds(pl.multiple_of(qd * CHUNK, CHUNK), CHUNK)
            plane_wait[g, j] = send(
                part.at[lo:hi, there, :], plane_in.at[lo:hi, j], sp.at[g, j], rp.at[g, j], d
            )

    mine = pl.ds(pl.multiple_of(q * CHUNK, CHUNK), CHUNK)

    def block_id(slot):
        r0, r1 = SLOTS[slot]
        if r0 == r1:
            return (c + r0) % 4
        if slot in OPEN:
            return 8 + (c + r0) % 2
        return 4 + (c + r0) % 4

    def sum_plane(g):
        lo, hi = GROUPS[g]
        for j in plane_peers:
            plane_wait[g, j].wait_recv()
        for slot in range(lo, hi):
            plane_in[slot, 0] = part[slot, mine, :]
            terms = plane_in[slot].reshape(16 * CHUNK, 2 * VIRT)
            plane_sum[block_id(slot)] = dot_nn(pick, terms)

    to_partner.wait_recv()
    product(0)
    passed = []
    for n, ((way, flip), came) in enumerate(near_in.items()):
        src = chip(-side if way == flip else side) * 2 + (h + flip) % 2
        passed.append(pass_on(n, came, src))
    for cp in passed:
        cp.wait_recv()
    for slot in range(1, EARLY):
        product(slot)
    share_products(0)
    through = []
    for flip, came in far_in.items():
        came.wait_recv()
        src = chip(side) * 2 + (h + flip) % 2
        there = ((c + side + 8) % 4) * 2 + (h + flip) % 2
        through.append(send(also.at[src], rows.at[there, other], st.at[flip], rt.at[flip], buddy))
    passed = []
    for flip, came in enumerate(through):
        passed.append(pass_on(4 + flip, came, chip(2) * 2 + (other + flip) % 2))
    for cp in passed:
        cp.wait_recv()
    mid = []
    for n, src in enumerate((c, chip(side))):
        mid.append(send(
            rows.at[pl.ds(src * 2, 2), h], also.at[pl.ds(src * 2, 2)], sm.at[n], rm.at[n], buddy
        ))
    for slot in range(EARLY, NBLK):
        product(slot)
    share_products(1)
    sum_plane(0)
    sum_plane(1)

    def share_of(k):
        return (
            pl.ds((k // 4) * 5, 5),
            slice(None),
            pl.ds(pl.multiple_of((k % 4) * 128, 128), 128),
        )

    z_wait = {}
    for dz, (d, zd) in z_peers.items():
        z_wait[dz] = send(plane_sum.at[share_of(zd)], z_in.at[dz], sz.at[dz], rz.at[dz], d)
    for dz in z_peers:
        z_wait[dz].wait_recv()

    hc = (z % 4) // 2
    va = vrow[mine, :]
    vb = energies[pl.ds(z % 2, 1), :]
    lanes = pl.ds(pl.multiple_of((z % 4) * 128, 128), 128)
    for t in range(5):
        b = (z // 4) * 5 + t
        s = plane_sum[b, :, lanes]
        for dz in z_peers:
            s += z_in[dz, t]
        first = b % 4
        lead = first * 2 + h
        second = jnp.where(b < 4, first, jnp.where(b < 8, (first + 1) % 4, first + 2))
        ea = rows[lead, h, VIRT:, 0:128].astype(F32)
        eb = rows[second * 2 + hc, h, VIRT:, 0:128].astype(F32)
        z_amps[b, :, lanes] = (s / ((va - ea) + (vb - eb))).astype(BF16)
    y_wait = {}
    for dz, (d, _) in z_peers.items():
        y_wait[dz] = send(
            z_amps.at[share_of(z)], z_amps.at[share_of(z)], sy.at[dz], ry.at[dz], d
        )
    for dz in z_peers:
        y_wait[dz].wait_recv()

    here = pl.ds(pl.multiple_of(h * VIRT + q * CHUNK, CHUNK), CHUNK)
    for slot in range(NBLK - 1):
        amps[slot, here, :] = z_amps[block_id(slot)]
    g_wait = {}
    for g, (lo, hi) in enumerate(SPREADS):
        piece = amps.at[lo:hi, here, :]
        g_wait[g, 0] = send(piece, piece, sh.at[g, 0], rh.at[g, 0], partner)
        for j, (d, _) in plane_peers.items():
            g_wait[g, j] = send(piece, piece, sg.at[g, j], rg.at[g, j], d)

    def collect(g):
        lo, hi = SPREADS[g]
        out = [g_wait[g, 0]]
        for j in plane_peers:
            dx, dy = j // 4, j % 4
            src_q = ((x + 4 - dx) % 4) * 4 + (y + 4 - dy) % 4
            g_wait[g, j].wait_recv()
            piece = amps.at[lo:hi, pl.ds(pl.multiple_of(h * VIRT + src_q * CHUNK, CHUNK), CHUNK), :]
            out.append(send(piece, piece, sh.at[g, j], rh.at[g, j], partner))
        for cp in out:
            cp.wait_recv()

    def lay(n, slot, as_is):
        @pl.when(as_is)
        def _():
            turned[n] = amps[slot]

        @pl.when(jnp.logical_not(as_is))
        def _():
            turned[n] = amps[slot].T

    def gamma_rows(factors, hr, target, weights):
        span = pl.ds(pl.multiple_of(hr * VIRT, VIRT), VIRT)
        row_chip, send_to = target
        ro = row_chip * 2 + hr
        for k in (0, 1):
            acc = None
            for dot, ref, co in factors:
                for hcol in range(2):
                    half = slice(hcol * VIRT, (hcol + 1) * VIRT)
                    block = ref[span, half] if dot is dot_nn else ref[half, span]
                    src = co * 2 + hcol
                    term = dot(block, rows[src, h, 0:VIRT] if k == 0 else also[src, 0:VIRT])
                    acc = term if acc is None else acc + term
            out = acc.astype(BF16)
            m = rows[ro, h, 0:VIRT] if k == 0 else also[ro, 0:VIRT]
            weights[k] += jnp.sum(out.astype(F32) * m.astype(F32), axis=0, keepdims=True)
            t = o if k == 0 else buddy_o
            cols = pl.ds(pl.multiple_of(t * COLS, COLS), COLS)
            if send_to is None:
                gamma[:, cols] = out
            else:
                n, d = send_to
                gout[n + k] = out
                b_wait.append(send(gout.at[n + k], gamma.at[:, cols], sb.at[n + k], rb.at[n + k], d))

    b_wait = []
    weights = [jnp.zeros((1, COLS), F32), jnp.zeros((1, COLS), F32)]
    also_in.wait_recv()
    for cp in mid:
        cp.wait_recv()
    collect(0)
    lay(0, 3 + h, h == 1)
    lay(1, 6 + h, h == 0)
    lay(2, 5, chip(side) < 2)
    factors = (
        (dot_nn, turned.at[0], c),
        (dot_nn, amps.at[1 + h], chip(side)),
        (dot_nn, turned.at[1], chip(2)),
        (dot_nn, turned.at[2], chip(-side)),
    )
    for flip in (0, 1):
        hr = (h + flip) % 2
        gamma_rows(factors, hr, (chip(side), (flip * 2, near[0, flip][0])), weights)
    collect(1)
    collect(2)
    lay(3, 8, c < 2)
    factors = (
        (dot_nn, amps.at[0], c),
        (dot_nn, amps.at[3], chip(1)),
        (dot_nn, turned.at[3], chip(2)),
        (dot_tn, amps.at[4], chip(3)),
    )
    gamma_rows(factors, other, (c, (4, partner)), weights)
    gamma_rows(factors, h, (c, None), weights)

    for k in (0, 1):
        wmine[k * 8 : k * 8 + 8, :] = jnp.broadcast_to(weights[k], (8, COLS))
        wall[o, k * 8 : k * 8 + 8, :] = jnp.broadcast_to(weights[k], (8, COLS))
    w_wait = [
        send(wmine, wall.at[o], sw.at[n], rw.at[n], d) for n, d in enumerate(everyone)
    ]
    for cp in w_wait:
        cp.wait_recv()
    for t in range(8):
        cols = slice(t * COLS, (t + 1) * COLS)
        pair = ((t // 2 + 2 * (t % 2) - 1) % 4) * 2 + 1 - t % 2
        w = wall[t, 0:1, :] + wall[pair, 8:9, :]
        for i in range(3):
            for j in range(3):
                n = 3 * i + j
                virial[n : n + 1, cols] = where[i : i + 1, cols] * where[j : j + 1, cols] * w
    for cp in b_wait:
        cp.wait_recv()
    for cp in sent:
        cp.wait_send()


def body(coeffs, occ_energy, virt_energy, screen, owner, positions):
    occ_dev, virt, aux_dev = coeffs.shape
    energies = jnp.concatenate(
        [virt_energy.reshape(2, 128), jnp.broadcast_to(occ_energy[:, None], (1, 128))]
    ).astype(F32)
    vmem = pl.BlockSpec(memory_space=pltpu.VMEM)
    smem = pl.BlockSpec(memory_space=pltpu.SMEM)
    dma = pltpu.SemaphoreType.DMA
    gamma, virial = pl.pallas_call(
        kernel,
        out_shape=(
            jax.ShapeDtypeStruct((VIRT, aux_dev), BF16),
            jax.ShapeDtypeStruct((9, aux_dev), F32),
        ),
        in_specs=[smem, smem, pl.BlockSpec(memory_space=pl.ANY), vmem, vmem],
        out_specs=(vmem, vmem),
        scratch_shapes=[
            pltpu.VMEM((8, VIRT, COLS), BF16),
            pltpu.VMEM((6, VIRT + TAIL, COLS), BF16),
            pltpu.VMEM((8, 2, VIRT + TAIL, COLS), BF16),
            pltpu.VMEM((8, VIRT + TAIL, COLS), BF16),
            pltpu.VMEM((VIRT, 128), F32),
            pltpu.VMEM((NBLK, VIRT, 2 * VIRT), BF16),
            pltpu.VMEM((NBLK, 16, CHUNK, 2 * VIRT), BF16),
            pltpu.VMEM((NBLK, CHUNK, 2 * VIRT), F32),
            pltpu.VMEM((8, 5, CHUNK, 128), F32),
            pltpu.VMEM((NBLK, CHUNK, 2 * VIRT), BF16),
            pltpu.VMEM((NBLK, 2 * VIRT, 2 * VIRT), BF16),
            pltpu.VMEM((4, 2 * VIRT, 2 * VIRT), BF16),
            pltpu.VMEM((6, VIRT, COLS), BF16),
            pltpu.VMEM((16, COLS), F32),
            pltpu.VMEM((8, 16, COLS), F32),
            pltpu.VMEM((8, aux_dev), F32),
            dma((8,)), dma((6,)), dma((6,)), dma((2,)), dma((2,)), dma((2,)), dma((2,)),
            dma((6,)), dma((6,)), dma((2,)), dma((2,)),
            dma((2, 16)), dma((2, 16)), dma((8,)), dma((8,)), dma((8,)), dma((8,)),
            dma((3, 16)), dma((3, 16)), dma((3, 16)), dma((3, 16)),
            dma((6,)), dma((6,)), dma((7,)), dma((7,)),
        ],
        compiler_params=pltpu.CompilerParams(
            collective_id=0, has_side_effects=True, vmem_limit_bytes=60 * 1024 * 1024
        ),
    )(screen, owner, coeffs.reshape(VIRT, aux_dev), energies, positions)
    return gamma.reshape(occ_dev, virt, aux_dev), virial


def solution(mesh):
    placed = (P("occ", None, "aux"), P("occ"), P(), P("occ", "aux"), P("aux"), P())
    return jax.shard_map(
        body,
        mesh=mesh,
        in_specs=placed,
        out_specs=(P("occ", None, "aux"), P(None, "aux")),
        check_vma=False,
    )
```

time: 195 us -> 177 us (0.908)
  Pallas kernels: 183 us -> 171 us
  local copies, waits for them, and re-layouts: 10.4 us -> 3.88 us
    pallas_call x1, Pallas kernels: 183 us -> 171 us  [body(): pl.pallas_call(kernel, out_shape=(jax.ShapeDtypeStruct((VIRT, aux_dev), B...]
    broadcast_in_dim x4 -> x0, local copies, waits for them, and re-layouts: 4.6 us -> none  [the longest x1 1.41 us: body(): vrow = jnp.broadcast_to(virt_f[:, None], (VIRT, 128))]
    unnamed x6 -> x4, local copies, waits for them, and re-layouts: 4.57 us -> 3.88 us
where the time goes in v2:
time: 177 us
  Pallas kernels  171 us (97%)
  local copies, waits for them, and re-layouts  3.88 us (2%)
    pallas_call x1, Pallas kernels, body(): pl.pallas_call(kernel, out_shape=(jax.ShapeDtypeStruct((VIRT, aux_dev), B...  171 us
    unnamed x4, local copies, waits for them, and re-layouts  3.88 us

profile of v2, /device:TPU:1, one launch (start us, length us, event | category | flops | bytes accessed | tf_op | source)
XLA Modules:
  0.0 177.3 jit_solution(4097272417023504379)
XLA Ops:
  1.3 1.2 pad_convert_fusion.energies
  2.5 170.9 %shard_map.77 = (bf16[256,4096]{1,0:T(8,128)(2,1)}, f32[9,4096]{1,0:T(8,128)}) custom-call(s32[1,32]{1,0:T(1,128)} %screen.1, s32[32]{0:T(128)} %owner.1, bf16[256,4096]{1,0:T(8,128)(2,1)} %bitcast.5, f32[3,128]{1,0:T(4,128)} %pad_convert_fusion.energies, f32[3,128]{1,0:T(4,128)} %positions.1), custom_call_target="tpu_custom_call" | custom-call | tf_op jit(solution)/shard_map/pallas_call | solution.py:374
  173.4 0.0 copy-start
  173.4 3.2 %copy.11 = bf16[1,256,4096]{2,1,0:T(8,128)(2,1)} copy(bf16[1,256,4096]{2,1,0:T(8,128)(2,1)} %bitcast.6) | data formatting | bytes 4194304
  176.6 0.0 copy-done
  176.6 0.7 copy.12
Async XLA Ops:
  173.4 3.2 %copy-start = (f32[9,4096]{1,0:T(8,128)S(1)}, f32[9,4096]{1,0:T(8,128)}, u32[]{:S(2)}) copy-start(f32[9,4096]{1,0:T(8,128)} %get-tuple-element.9) | copy-start | bytes 442372

commit v3 on v2

--- a/solution.py
+++ b/solution.py
@@ -14,12 +14,14 @@
 TAIL = 16
 CHUNK = 16
 NBLK = 10
+PARTS = (slice(0, 256),)
 EARLY = 6
 
 SLOTS = ((0, 0), (1, 1), (3, 3), (0, 1), (3, 0), (1, 3), (1, 2), (2, 3), (0, 2), (2, 2))
 OPEN = (5, 8)
 GROUPS = ((0, EARLY), (EARLY, NBLK))
-SPREADS = ((1, 8), (8, 9), (0, 1))
+KEPT = (1, 2, 3, 4, 5, 6, 7, 0, 8)
+SPREADS = ((0, 7), (7, 9))
 
 
 def dot_nt(a, b):
@@ -37,9 +39,9 @@
 def kernel(
     screen, owner, coeffs, energies, positions,
     gamma, virial,
-    raw, slabs, rows, also, vrow, part, plane_in, plane_sum, z_in, z_amps, amps, turned, gout,
+    raw, slabs, rows, also, levels, vrow, part, plane_in, plane_sum, plane_out, z_in, z_amps, amps, turned, gout,
     wmine, wall, where,
-    sl, sa, ra, sr, rr, st, rt, sf, rf, sm, rm, sp, rp, sz, rz, sy, ry, sg, rg, sh, rh, sb, rb, sw, rw,
+    se, re, sl, sa, ra, sr, rr, st, rt, sf, rf, sm, rm, sp, rp, sz, rz, sy, ry, sg, rg, sh, rh, sb, rb, sw, rw,
 ):
     o = lax.axis_index("occ")
     a = lax.axis_index("aux")
@@ -105,7 +107,7 @@
         loads.append(pltpu.make_async_copy(coeffs.at[:, cols], raw.at[n], sl.at[n]))
         loads[n].start()
 
-    energy = jnp.broadcast_to(energies[2:3, :], (TAIL, 128)).astype(BF16)
+    levels[o] = jnp.broadcast_to(energies[2:3, :], (TAIL, 128)).astype(BF16)
     near_in, far_in = {}, {}
     for n, t in enumerate(order):
         to = slabs.at[n] if n < 6 else rows.at[o, t % 2]
@@ -114,17 +116,23 @@
             cols = slice(b * ABLK, (b + 1) * ABLK)
             keep = screen[0, t * (COLS // ABLK) + b].astype(F32)
             kept = raw[n, :, cols] * jnp.full((VIRT, ABLK), keep, F32).astype(BF16)
-            to[0:VIRT, cols] = kept
-            to[VIRT:, cols] = energy
+            to[:, cols] = kept
             if n == 3:
-                also[o, 0:VIRT, cols] = kept
+                also[o, :, cols] = kept
         if n == 0:
             pl.semaphore_wait(barrier, len(greet))
         if n < 4:
             key = list(near)[n]
             near_in[key] = send(slabs.at[n], rows.at[o, t % 2], sa.at[n], ra.at[n], near[key][0])
         elif n < 6:
-            far_in[n - 4] = send(slabs.at[n], also.at[o], sr.at[n - 4], rr.at[n - 4], far[n - 4][0])
+            for p, span in enumerate(PARTS):
+                k = (n - 4) * 2 + p
+                far_in[n - 4, p] = send(
+                    slabs.at[n, span], also.at[o, span], sr.at[k], rr.at[k], far[n - 4][0]
+                )
+    level_in = [
+        send(levels.at[o], levels.at[o], se.at[n], re.at[n], d) for n, d in enumerate(everyone)
+    ]
     to_partner = send(rows.at[o], rows.at[o], sa.at[4], ra.at[4], partner)
     also_in = send(slabs.at[0], also.at[o], sa.at[5], ra.at[5], partner)
 
@@ -148,13 +156,13 @@
             first, second = jnp.minimum(first, second), jnp.maximum(first, second)
         lead = first * 2 + h
         for hc in (0, 1):
-            s = dot_nt(rows[lead, 0, 0:VIRT], rows[second * 2 + hc, 0, 0:VIRT])
-            s += dot_nt(rows[lead, 1, 0:VIRT], rows[second * 2 + hc, 1, 0:VIRT])
+            s = dot_nt(rows[lead, 0], rows[second * 2 + hc, 0])
+            s += dot_nt(rows[lead, 1], rows[second * 2 + hc, 1])
             part[slot, :, hc * VIRT : (hc + 1) * VIRT] = s.astype(BF16)
 
-    def pass_on(n, came, src):
+    def pass_on(n, came, src, span=slice(0, VIRT)):
         came.wait_recv()
-        piece = rows.at[src, h]
+        piece = rows.at[src, h, span]
         return send(piece, piece, sf.at[n], rf.at[n], partner)
 
     plane_wait = {}
@@ -184,7 +192,9 @@
         for slot in range(lo, hi):
             plane_in[slot, 0] = part[slot, mine, :]
             terms = plane_in[slot].reshape(16 * CHUNK, 2 * VIRT)
-            plane_sum[block_id(slot)] = dot_nn(pick, terms)
+            s = dot_nn(pick, terms)
+            plane_sum[block_id(slot)] = s
+            plane_out[block_id(slot)] = s.astype(BF16)
 
     to_partner.wait_recv()
     product(0)
@@ -197,27 +207,34 @@
     for slot in range(1, EARLY):
         product(slot)
     share_products(0)
-    through = []
-    for flip, came in far_in.items():
-        came.wait_recv()
-        src = chip(side) * 2 + (h + flip) % 2
-        there = ((c + side + 8) % 4) * 2 + (h + flip) % 2
-        through.append(send(also.at[src], rows.at[there, other], st.at[flip], rt.at[flip], buddy))
+    through = {}
+    for p, span in enumerate(PARTS):
+        for flip in (0, 1):
+            far_in[flip, p].wait_recv()
+            src = chip(side) * 2 + (h + flip) % 2
+            k = flip * 2 + p
+            through[flip, p] = send(
+                also.at[src, span], rows.at[src, other, span], st.at[k], rt.at[k], buddy
+            )
     passed = []
-    for flip, came in enumerate(through):
-        passed.append(pass_on(4 + flip, came, chip(2) * 2 + (other + flip) % 2))
+    for (flip, p), came in through.items():
+        src = chip(2) * 2 + (other + flip) % 2
+        passed.append(pass_on(4 + flip * 2 + p, came, src, PARTS[p]))
     for cp in passed:
         cp.wait_recv()
-    mid = []
-    for n, src in enumerate((c, chip(side))):
-        mid.append(send(
+
+    def lend(n, src):
+        return send(
             rows.at[pl.ds(src * 2, 2), h], also.at[pl.ds(src * 2, 2)], sm.at[n], rm.at[n], buddy
-        ))
-    for slot in range(EARLY, NBLK):
-        product(slot)
-    share_products(1)
-    sum_plane(0)
-    sum_plane(1)
+        )
+
+    mid = [lend(0, c)]
+    for g in (1,):
+        for slot in range(*GROUPS[g]):
+            product(slot)
+        share_products(g)
+    for g in (0, 1):
+        sum_plane(g)
 
     def share_of(k):
         return (
@@ -228,10 +245,12 @@
 
     z_wait = {}
     for dz, (d, zd) in z_peers.items():
-        z_wait[dz] = send(plane_sum.at[share_of(zd)], z_in.at[dz], sz.at[dz], rz.at[dz], d)
+        z_wait[dz] = send(plane_out.at[share_of(zd)], z_in.at[dz], sz.at[dz], rz.at[dz], d)
     for dz in z_peers:
         z_wait[dz].wait_recv()
 
+    for cp in level_in:
+        cp.wait_recv()
     hc = (z % 4) // 2
     va = vrow[mine, :]
     vb = energies[pl.ds(z % 2, 1), :]
@@ -240,41 +259,74 @@
         b = (z // 4) * 5 + t
         s = plane_sum[b, :, lanes]
         for dz in z_peers:
-            s += z_in[dz, t]
+            s += z_in[dz, t].astype(F32)
         first = b % 4
         lead = first * 2 + h
         second = jnp.where(b < 4, first, jnp.where(b < 8, (first + 1) % 4, first + 2))
-        ea = rows[lead, h, VIRT:, 0:128].astype(F32)
-        eb = rows[second * 2 + hc, h, VIRT:, 0:128].astype(F32)
+        ea = levels[lead].astype(F32)
+        eb = levels[second * 2 + hc].astype(F32)
         z_amps[b, :, lanes] = (s / ((va - ea) + (vb - eb))).astype(BF16)
     y_wait = {}
     for dz, (d, _) in z_peers.items():
         y_wait[dz] = send(
             z_amps.at[share_of(z)], z_amps.at[share_of(z)], sy.at[dz], ry.at[dz], d
         )
+    mid.append(lend(1, chip(side)))
     for dz in z_peers:
         y_wait[dz].wait_recv()
 
     here = pl.ds(pl.multiple_of(h * VIRT + q * CHUNK, CHUNK), CHUNK)
-    for slot in range(NBLK - 1):
-        amps[slot, here, :] = z_amps[block_id(slot)]
-    g_wait = {}
-    for g, (lo, hi) in enumerate(SPREADS):
-        piece = amps.at[lo:hi, here, :]
-        g_wait[g, 0] = send(piece, piece, sh.at[g, 0], rh.at[g, 0], partner)
-        for j, (d, _) in plane_peers.items():
-            g_wait[g, j] = send(piece, piece, sg.at[g, j], rg.at[g, j], d)
+    for k, slot in enumerate(KEPT):
+        amps[k, here, :] = z_amps[block_id(slot)]
+
+    def piece(g, half, i, j):
+        i, j = (i, j) if half == 0 else (j, i)
+        src_q = ((x + 4 - i) % 4) * 4 + (y + 4 - j) % 4
+        rows_ = pl.ds(pl.multiple_of(h * VIRT + src_q * CHUNK, CHUNK), CHUNK)
+        return amps.at[slice(*SPREADS[g]), rows_, half * VIRT : (half + 1) * VIRT]
+
+    def peer(half, i, j):
+        i, j = (i, j) if half == 0 else (j, i)
+        return plane_peers[i * 4 + j][0]
+
+    g_wait, h_wait = {}, {0: [], 1: []}
+
+    def spread(g, half, i):
+        for j in (1, 3, 2):
+            k = i * 4 + j
+            g_wait[g, half, k] = send(
+                piece(g, half, i, 0), piece(g, half, i, 0), sg.at[g, half, k], rg.at[g, half, k], peer(half, 0, j)
+            )
+
+    def to_other(g, half, i, j):
+        k = i * 4 + j
+        ref = piece(g, half, i, j)
+        h_wait[g].append(send(ref, ref, sh.at[g, half, k], rh.at[g, half, k], partner))
+
+    def begin(g):
+        for i in (1, 3, 2):
+            for half in (0, 1):
+                k = i * 4
+                ref = piece(g, half, 0, 0)
+                g_wait[g, half, k] = send(ref, ref, sg.at[g, half, k], rg.at[g, half, k], peer(half, i, 0))
+        for half in (0, 1):
+            spread(g, half, 0)
+            to_other(g, half, 0, 0)
+
+    def relay(g):
+        for i in (1, 3, 2):
+            for half in (0, 1):
+                g_wait[g, half, i * 4].wait_recv()
+                spread(g, half, i)
+                to_other(g, half, i, 0)
 
     def collect(g):
-        lo, hi = SPREADS[g]
-        out = [g_wait[g, 0]]
-        for j in plane_peers:
-            dx, dy = j // 4, j % 4
-            src_q = ((x + 4 - dx) % 4) * 4 + (y + 4 - dy) % 4
-            g_wait[g, j].wait_recv()
-            piece = amps.at[lo:hi, pl.ds(pl.multiple_of(h * VIRT + src_q * CHUNK, CHUNK), CHUNK), :]
-            out.append(send(piece, piece, sh.at[g, j], rh.at[g, j], partner))
-        for cp in out:
+        for i in (0, 1, 3, 2):
+            for j in (1, 3, 2):
+                for half in (0, 1):
+                    g_wait[g, half, i * 4 + j].wait_recv()
+                    to_other(g, half, i, j)
+        for cp in h_wait[g]:
             cp.wait_recv()
 
     def lay(n, slot, as_is):
@@ -297,10 +349,10 @@
                     half = slice(hcol * VIRT, (hcol + 1) * VIRT)
                     block = ref[span, half] if dot is dot_nn else ref[half, span]
                     src = co * 2 + hcol
-                    term = dot(block, rows[src, h, 0:VIRT] if k == 0 else also[src, 0:VIRT])
+                    term = dot(block, rows[src, h] if k == 0 else also[src])
                     acc = term if acc is None else acc + term
             out = acc.astype(BF16)
-            m = rows[ro, h, 0:VIRT] if k == 0 else also[ro, 0:VIRT]
+            m = rows[ro, h] if k == 0 else also[ro]
             weights[k] += jnp.sum(out.astype(F32) * m.astype(F32), axis=0, keepdims=True)
             t = o if k == 0 else buddy_o
             cols = pl.ds(pl.multiple_of(t * COLS, COLS), COLS)
@@ -309,36 +361,51 @@
             else:
                 n, d = send_to
                 gout[n + k] = out
-                b_wait.append(send(gout.at[n + k], gamma.at[:, cols], sb.at[n + k], rb.at[n + k], d))
+                ready.append((n + k, cols, d))
+                if n == 0:
+                    send_ready()
+
+    def send_ready():
+        for n, cols, d in ready:
+            b_wait.append(send(gout.at[n], gamma.at[:, cols], sb.at[n], rb.at[n], d))
+        ready.clear()
+
+    ready = []
 
     b_wait = []
     weights = [jnp.zeros((1, COLS), F32), jnp.zeros((1, COLS), F32)]
+    begin(0)
+    relay(0)
+    begin(1)
+    relay(1)
     also_in.wait_recv()
     for cp in mid:
         cp.wait_recv()
     collect(0)
-    lay(0, 3 + h, h == 1)
-    lay(1, 6 + h, h == 0)
-    lay(2, 5, chip(side) < 2)
+    lay(0, 2 + h, h == 1)
+    lay(1, 5 + h, h == 0)
+    lay(2, 4, chip(side) < 2)
     factors = (
         (dot_nn, turned.at[0], c),
-        (dot_nn, amps.at[1 + h], chip(side)),
+        (dot_nn, amps.at[h], chip(side)),
         (dot_nn, turned.at[1], chip(2)),
         (dot_nn, turned.at[2], chip(-side)),
     )
     for flip in (0, 1):
         hr = (h + flip) % 2
         gamma_rows(factors, hr, (chip(side), (flip * 2, near[0, flip][0])), weights)
+    later = [*ready]
+    ready.clear()
     collect(1)
-    collect(2)
     lay(3, 8, c < 2)
     factors = (
-        (dot_nn, amps.at[0], c),
-        (dot_nn, amps.at[3], chip(1)),
+        (dot_nn, amps.at[7], c),
+        (dot_nn, amps.at[2], chip(1)),
         (dot_nn, turned.at[3], chip(2)),
-        (dot_tn, amps.at[4], chip(3)),
+        (dot_tn, amps.at[3], chip(3)),
     )
     gamma_rows(factors, other, (c, (4, partner)), weights)
+    send_ready()
     gamma_rows(factors, h, (c, None), weights)
 
     for k in (0, 1):
@@ -347,6 +414,8 @@
     w_wait = [
         send(wmine, wall.at[o], sw.at[n], rw.at[n], d) for n, d in enumerate(everyone)
     ]
+    ready.extend(later)
+    send_ready()
     for cp in w_wait:
         cp.wait_recv()
     for t in range(8):
@@ -381,25 +450,27 @@
         out_specs=(vmem, vmem),
         scratch_shapes=[
             pltpu.VMEM((8, VIRT, COLS), BF16),
-            pltpu.VMEM((6, VIRT + TAIL, COLS), BF16),
-            pltpu.VMEM((8, 2, VIRT + TAIL, COLS), BF16),
-            pltpu.VMEM((8, VIRT + TAIL, COLS), BF16),
+            pltpu.VMEM((6, VIRT, COLS), BF16),
+            pltpu.VMEM((8, 2, VIRT, COLS), BF16),
+            pltpu.VMEM((8, VIRT, COLS), BF16),
+            pltpu.VMEM((8, TAIL, 128), BF16),
             pltpu.VMEM((VIRT, 128), F32),
             pltpu.VMEM((NBLK, VIRT, 2 * VIRT), BF16),
             pltpu.VMEM((NBLK, 16, CHUNK, 2 * VIRT), BF16),
             pltpu.VMEM((NBLK, CHUNK, 2 * VIRT), F32),
-            pltpu.VMEM((8, 5, CHUNK, 128), F32),
             pltpu.VMEM((NBLK, CHUNK, 2 * VIRT), BF16),
-            pltpu.VMEM((NBLK, 2 * VIRT, 2 * VIRT), BF16),
+            pltpu.VMEM((8, 5, CHUNK, 128), BF16),
+            pltpu.VMEM((NBLK, CHUNK, 2 * VIRT), BF16),
+            pltpu.VMEM((NBLK - 1, 2 * VIRT, 2 * VIRT), BF16),
             pltpu.VMEM((4, 2 * VIRT, 2 * VIRT), BF16),
             pltpu.VMEM((6, VIRT, COLS), BF16),
             pltpu.VMEM((16, COLS), F32),
             pltpu.VMEM((8, 16, COLS), F32),
             pltpu.VMEM((8, aux_dev), F32),
-            dma((8,)), dma((6,)), dma((6,)), dma((2,)), dma((2,)), dma((2,)), dma((2,)),
-            dma((6,)), dma((6,)), dma((2,)), dma((2,)),
-            dma((2, 16)), dma((2, 16)), dma((8,)), dma((8,)), dma((8,)), dma((8,)),
-            dma((3, 16)), dma((3, 16)), dma((3, 16)), dma((3, 16)),
+            dma((7,)), dma((7,)), dma((8,)), dma((6,)), dma((6,)), dma((4,)), dma((4,)), dma((4,)), dma((4,)),
+            dma((8,)), dma((8,)), dma((2,)), dma((2,)),
+            dma((3, 16)), dma((3, 16)), dma((8,)), dma((8,)), dma((8,)), dma((8,)),
+            dma((2, 2, 16)), dma((2, 2, 16)), dma((2, 2, 16)), dma((2, 2, 16)),
             dma((6,)), dma((6,)), dma((7,)), dma((7,)),
         ],
         compiler_params=pltpu.CompilerParams(

time: 177 us -> 157 us (0.89)
  Pallas kernels: 171 us -> 150 us
    pallas_call x1, Pallas kernels: 171 us -> 150 us  [body(): pl.pallas_call(kernel, out_shape=(jax.ShapeDtypeStruct((VIRT, aux_dev), B...]
where the time goes in v3:
time: 157 us
  Pallas kernels  150 us (96%)
  local copies, waits for them, and re-layouts  3.88 us (2%)
    pallas_call x1, Pallas kernels, body(): pl.pallas_call(kernel, out_shape=(jax.ShapeDtypeStruct((VIRT, aux_dev), B...  150 us
    unnamed x4, local copies, waits for them, and re-layouts  3.88 us

profile of v3, /device:TPU:1, one launch (start us, length us, event | category | flops | bytes accessed | tf_op | source)
XLA Modules:
  0.0 156.7 jit_solution(13639630289674548730)
XLA Ops:
  1.3 1.2 pad_convert_fusion.energies
  2.5 150.3 %shard_map.77 = (bf16[256,4096]{1,0:T(8,128)(2,1)}, f32[9,4096]{1,0:T(8,128)}) custom-call(s32[1,32]{1,0:T(1,128)} %screen.1, s32[32]{0:T(128)} %owner.1, bf16[256,4096]{1,0:T(8,128)(2,1)} %bitcast.5, f32[3,128]{1,0:T(4,128)} %pad_convert_fusion.energies, f32[3,128]{1,0:T(4,128)} %positions.1), custom_call_target="tpu_custom_call" | custom-call | tf_op jit(solution)/shard_map/pallas_call | solution.py:443
  152.8 0.0 copy-start
  152.8 3.2 %copy.11 = bf16[1,256,4096]{2,1,0:T(8,128)(2,1)} copy(bf16[1,256,4096]{2,1,0:T(8,128)(2,1)} %bitcast.6) | data formatting | bytes 4194304
  156.0 0.0 copy-done
  156.0 0.7 copy.12
Async XLA Ops:
  152.8 3.2 %copy-start = (f32[9,4096]{1,0:T(8,128)S(1)}, f32[9,4096]{1,0:T(8,128)}, u32[]{:S(2)}) copy-start(f32[9,4096]{1,0:T(8,128)} %get-tuple-element.9) | copy-start | bytes 442372

commit v4 on v3

--- a/solution.py
+++ b/solution.py
@@ -298,10 +298,9 @@
                 piece(g, half, i, 0), piece(g, half, i, 0), sg.at[g, half, k], rg.at[g, half, k], peer(half, 0, j)
             )
 
-    def to_other(g, half, i, j):
-        k = i * 4 + j
-        ref = piece(g, half, i, j)
-        h_wait[g].append(send(ref, ref, sh.at[g, half, k], rh.at[g, half, k], partner))
+    def to_other(g, n, rows_, cols):
+        ref = amps.at[slice(*SPREADS[g]), rows_, cols]
+        h_wait[g].append(send(ref, ref, sh.at[g, n], rh.at[g, n], partner))
 
     def begin(g):
         for i in (1, 3, 2):
@@ -311,21 +310,24 @@
                 g_wait[g, half, k] = send(ref, ref, sg.at[g, half, k], rg.at[g, half, k], peer(half, i, 0))
         for half in (0, 1):
             spread(g, half, 0)
-            to_other(g, half, 0, 0)
 
     def relay(g):
         for i in (1, 3, 2):
             for half in (0, 1):
                 g_wait[g, half, i * 4].wait_recv()
                 spread(g, half, i)
-                to_other(g, half, i, 0)
 
     def collect(g):
         for i in (0, 1, 3, 2):
             for j in (1, 3, 2):
-                for half in (0, 1):
-                    g_wait[g, half, i * 4 + j].wait_recv()
-                    to_other(g, half, i, j)
+                g_wait[g, 0, i * 4 + j].wait_recv()
+            first = pl.multiple_of(h * VIRT + ((x + 4 - i) % 4) * 4 * CHUNK, 4 * CHUNK)
+            to_other(g, i, pl.ds(first, 4 * CHUNK), slice(0, VIRT))
+        for i in (0, 1, 3, 2):
+            for j in (1, 3, 2):
+                g_wait[g, 1, i * 4 + j].wait_recv()
+        own = pl.ds(pl.multiple_of(h * VIRT, VIRT), VIRT)
+        to_other(g, 4, own, slice(VIRT, 2 * VIRT))
         for cp in h_wait[g]:
             cp.wait_recv()
 
@@ -432,6 +434,17 @@
         cp.wait_send()
 
 
+def write_out(gamma_in, virial_in, gamma, virial, sem):
+    copies = [
+        pltpu.make_async_copy(gamma_in, gamma, sem.at[0]),
+        pltpu.make_async_copy(virial_in, virial, sem.at[1]),
+    ]
+    for cp in copies:
+        cp.start()
+    for cp in copies:
+        cp.wait()
+
+
 def body(coeffs, occ_energy, virt_energy, screen, owner, positions):
     occ_dev, virt, aux_dev = coeffs.shape
     energies = jnp.concatenate(
@@ -442,11 +455,8 @@
     dma = pltpu.SemaphoreType.DMA
     gamma, virial = pl.pallas_call(
         kernel,
-        out_shape=(
-            jax.ShapeDtypeStruct((VIRT, aux_dev), BF16),
-            jax.ShapeDtypeStruct((9, aux_dev), F32),
-        ),
-        in_specs=[smem, smem, pl.BlockSpec(memory_space=pl.ANY), vmem, vmem],
+        out_shape=(pltpu.VMEM((VIRT, aux_dev), BF16), pltpu.VMEM((9, aux_dev), F32)),
+        in_specs=[smem, smem, pl.BlockSpec(memory_space=pltpu.HBM), vmem, vmem],
         out_specs=(vmem, vmem),
         scratch_shapes=[
             pltpu.VMEM((8, VIRT, COLS), BF16),
@@ -470,13 +480,24 @@
             dma((7,)), dma((7,)), dma((8,)), dma((6,)), dma((6,)), dma((4,)), dma((4,)), dma((4,)), dma((4,)),
             dma((8,)), dma((8,)), dma((2,)), dma((2,)),
             dma((3, 16)), dma((3, 16)), dma((8,)), dma((8,)), dma((8,)), dma((8,)),
-            dma((2, 2, 16)), dma((2, 2, 16)), dma((2, 2, 16)), dma((2, 2, 16)),
+            dma((2, 2, 16)), dma((2, 2, 16)), dma((2, 5)), dma((2, 5)),
             dma((6,)), dma((6,)), dma((7,)), dma((7,)),
         ],
         compiler_params=pltpu.CompilerParams(
-            collective_id=0, has_side_effects=True, vmem_limit_bytes=60 * 1024 * 1024
+            collective_id=0, has_side_effects=True, vmem_limit_bytes=64684032
         ),
     )(screen, owner, coeffs.reshape(VIRT, aux_dev), energies, positions)
+    gamma, virial = pl.pallas_call(
+        write_out,
+        out_shape=(
+            jax.ShapeDtypeStruct((VIRT, aux_dev), BF16),
+            jax.ShapeDtypeStruct((9, aux_dev), F32),
+        ),
+        in_specs=[pl.BlockSpec(memory_space=pl.ANY)] * 2,
+        out_specs=(pl.BlockSpec(memory_space=pl.ANY),) * 2,
+        scratch_shapes=[dma((2,))],
+        compiler_params=pltpu.CompilerParams(vmem_limit_bytes=1024 * 1024),
+    )(gamma, virial)
     return gamma.reshape(occ_dev, virt, aux_dev), virial
 
 

time: 157 us -> 152 us (0.968)
  local copies, waits for them, and re-layouts: 3.88 us -> 0 us
  Pallas kernels: 150 us -> 148 us
    unnamed x4 -> x0, local copies, waits for them, and re-layouts: 3.88 us -> none
    pallas_call x1 -> x2, Pallas kernels: 150 us -> 148 us  [the longest x1 146 us: body(): pl.pallas_call(kernel, out_shape=(pltpu.VMEM((VIRT, aux_dev), BF16), pltp...]
where the time goes in v4:
time: 152 us; the launch traced here: 150 us
  Pallas kernels  148 us (97%)
    pallas_call x1, Pallas kernels, body(): pl.pallas_call(kernel, out_shape=(pltpu.VMEM((VIRT, aux_dev), BF16), pltp...  146 us

profile of v4, /device:TPU:1, one launch (start us, length us, event | category | flops | bytes accessed | tf_op | source)
XLA Modules:
  0.0 150.4 jit_solution(13690189733884157878)
XLA Ops:
  1.3 1.2 pad_convert_fusion.energies
  2.5 146.4 %shard_map.77 = (bf16[256,4096]{1,0:T(8,128)(2,1)S(1)}, f32[9,4096]{1,0:T(8,128)S(1)}) custom-call(s32[1,32]{1,0:T(1,128)} %screen.1, s32[32]{0:T(128)} %owner.1, bf16[256,4096]{1,0:T(8,128)(2,1)} %bitcast.5, f32[3,128]{1,0:T(4,128)} %pad_convert_fusion.energies, f32[3,128]{1,0:T(4,128)} %positions.1), custom_call_target="tpu_custom_call" | custom-call | tf_op jit(solution)/shard_map/pallas_call | solution.py:456
  148.9 1.4 shard_map.78

commit v5 on v4

--- a/solution.py
+++ b/solution.py
@@ -19,7 +19,7 @@
 
 SLOTS = ((0, 0), (1, 1), (3, 3), (0, 1), (3, 0), (1, 3), (1, 2), (2, 3), (0, 2), (2, 2))
 OPEN = (5, 8)
-GROUPS = ((0, EARLY), (EARLY, NBLK))
+GROUPS = ((0, 1), (1, 3), (3, EARLY), (EARLY, 8), (8, NBLK))
 KEPT = (1, 2, 3, 4, 5, 6, 7, 0, 8)
 SPREADS = ((0, 7), (7, 9))
 
@@ -198,15 +198,17 @@
 
     to_partner.wait_recv()
     product(0)
+    share_products(0)
     passed = []
     for n, ((way, flip), came) in enumerate(near_in.items()):
         src = chip(-side if way == flip else side) * 2 + (h + flip) % 2
         passed.append(pass_on(n, came, src))
     for cp in passed:
         cp.wait_recv()
-    for slot in range(1, EARLY):
-        product(slot)
-    share_products(0)
+    for g in (1, 2):
+        for slot in range(*GROUPS[g]):
+            product(slot)
+        share_products(g)
     through = {}
     for p, span in enumerate(PARTS):
         for flip in (0, 1):
@@ -229,11 +231,11 @@
         )
 
     mid = [lend(0, c)]
-    for g in (1,):
+    for g in (3, 4):
         for slot in range(*GROUPS[g]):
             product(slot)
         share_products(g)
-    for g in (0, 1):
+    for g in range(len(GROUPS)):
         sum_plane(g)
 
     def share_of(k):
@@ -271,9 +273,9 @@
         y_wait[dz] = send(
             z_amps.at[share_of(z)], z_amps.at[share_of(z)], sy.at[dz], ry.at[dz], d
         )
-    mid.append(lend(1, chip(side)))
     for dz in z_peers:
         y_wait[dz].wait_recv()
+    mid.append(lend(1, chip(side)))
 
     here = pl.ds(pl.multiple_of(h * VIRT + q * CHUNK, CHUNK), CHUNK)
     for k, slot in enumerate(KEPT):
@@ -354,8 +356,6 @@
                     term = dot(block, rows[src, h] if k == 0 else also[src])
                     acc = term if acc is None else acc + term
             out = acc.astype(BF16)
-            m = rows[ro, h] if k == 0 else also[ro]
-            weights[k] += jnp.sum(out.astype(F32) * m.astype(F32), axis=0, keepdims=True)
             t = o if k == 0 else buddy_o
             cols = pl.ds(pl.multiple_of(t * COLS, COLS), COLS)
             if send_to is None:
@@ -366,6 +366,8 @@
                 ready.append((n + k, cols, d))
                 if n == 0:
                     send_ready()
+            m = rows[ro, h] if k == 0 else also[ro]
+            weights[k] += jnp.sum(out.astype(F32) * m.astype(F32), axis=0, keepdims=True)
 
     def send_ready():
         for n, cols, d in ready:
@@ -479,7 +481,7 @@
             pltpu.VMEM((8, aux_dev), F32),
             dma((7,)), dma((7,)), dma((8,)), dma((6,)), dma((6,)), dma((4,)), dma((4,)), dma((4,)), dma((4,)),
             dma((8,)), dma((8,)), dma((2,)), dma((2,)),
-            dma((3, 16)), dma((3, 16)), dma((8,)), dma((8,)), dma((8,)), dma((8,)),
+            dma((5, 16)), dma((5, 16)), dma((8,)), dma((8,)), dma((8,)), dma((8,)),
             dma((2, 2, 16)), dma((2, 2, 16)), dma((2, 5)), dma((2, 5)),
             dma((6,)), dma((6,)), dma((7,)), dma((7,)),
         ],

time: 152 us -> 147 us (0.967)
  Pallas kernels: 148 us -> 143 us
    pallas_call x1, Pallas kernels: 146 us -> 141 us  [body(): pl.pallas_call(kernel, out_shape=(pltpu.VMEM((VIRT, aux_dev), BF16), pltp...]
where the time goes in v5:
time: 147 us; the launch traced here: 145 us
  Pallas kernels  143 us (97%)
    pallas_call x1, Pallas kernels, body(): pl.pallas_call(kernel, out_shape=(pltpu.VMEM((VIRT, aux_dev), BF16), pltp...  141 us

profile of v5, /device:TPU:1, one launch (start us, length us, event | category | flops | bytes accessed | tf_op | source)
XLA Modules:
  0.0 145.3 jit_solution(4821395913403167582)
XLA Ops:
  1.3 1.2 pad_convert_fusion.energies
  2.5 141.3 %shard_map.77 = (bf16[256,4096]{1,0:T(8,128)(2,1)S(1)}, f32[9,4096]{1,0:T(8,128)S(1)}) custom-call(s32[1,32]{1,0:T(1,128)} %screen.1, s32[32]{0:T(128)} %owner.1, bf16[256,4096]{1,0:T(8,128)(2,1)} %bitcast.5, f32[3,128]{1,0:T(4,128)} %pad_convert_fusion.energies, f32[3,128]{1,0:T(4,128)} %positions.1), custom_call_target="tpu_custom_call" | custom-call | tf_op jit(solution)/shard_map/pallas_call | solution.py:458
  143.9 1.4 shard_map.78
